TPU v7x, 512 devices: a whole 4x8x8 slice. The times are simulated.
512 devices in a mesh: dp: 16 (over y, core), expert: 8 (over z), tensor: 4 (over x).
Axes of the slice: x: 4, y: 8, z: 8, core: 2. Of those that a mesh axis runs over, the one named last changes fastest.
Arguments:
- tokens: bfloat16 [8192, 4096], P(('dp', 'expert'), 'tensor'), may hold values from -6 to 6
- expert_ids: int32 [8192, 8], P(('dp', 'expert')), may hold values from 0 to 127, all different within a row; in each aligned block of 64 rows (0 to 63, 64 to 127, ...) at most 6 rows name the same one
- combine_weights: float32 [8192, 8], P(('dp', 'expert')), may hold values from 0.05 to 1
- topology: int32 [128, 12, 12], P(('dp', 'expert'), 'tensor'), may hold values from 0 to 31, all different within a row
- gate_blocks: bfloat16 [128, 12, 12, 128, 128], P(('dp', 'expert'), 'tensor'), may hold values from -0.15625 to 0.15625
- up_blocks: bfloat16 [128, 12, 12, 128, 128], P(('dp', 'expert'), 'tensor'), may hold values from -0.15625 to 0.15625
- down_blocks: bfloat16 [128, 12, 12, 128, 128], P(('dp', 'expert'), 'tensor'), may hold values from -0.25 to 0.25
Outputs:
- layer_out: bfloat16 [8192, 4096], P(('dp', 'expert'), 'tensor')
Inputs may be any that keep to these rules, and one draw needn't show every extreme that they name: `expert_ids`: in each aligned block of 64 tokens (the tokens of one index of dp+expert), no expert is named more than 6 times, a bound that some block reaches; a token names 8 different experts. `topology`: each row names 12 different blocks; every block is named by some row.
All inputs are finite; a program needn't handle non-finite values.
Results may differ from a plain program's by a relative error of at most 0.0058.
Values may be sent and summed in bfloat16 or wider, within the bound.
A program may use at most 128 MiB of HBM per device.

v0:
```python
import jax
import jax.numpy as jnp
from jax import lax
from jax.sharding import PartitionSpec as P

D = 4096
TOP = 8
BLK = 128


def slot_numbers(expert_ids, experts):
    flat_ids = expert_ids.reshape(-1)
    onehot = (flat_ids[:, None] == jnp.arange(experts, dtype=jnp.int32)[None, :]).astype(jnp.int32)
    before = jnp.cumsum(onehot, axis=0) - onehot
    return jnp.sum(before * onehot, axis=1).reshape(expert_ids.shape)


def combine_rows(flat_rows, target, combine_weights):
    total = jnp.zeros((target.shape[0], flat_rows.shape[1]), jnp.float32)
    for pick in range(target.shape[1]):
        chosen = jnp.take(flat_rows, target[:, pick], axis=0)
        total = total + combine_weights[:, pick][:, None] * chosen
    return total


def per_device(tokens, expert_ids, combine_weights, topology, gate_blocks, up_blocks, down_blocks):
    experts = lax.axis_size(("dp", "expert"))
    tok_rows = tokens.shape[0]
    capacity = min(tok_rows, 3 * tok_rows * TOP // (2 * experts))
    slot_index = slot_numbers(expert_ids, experts)
    target = expert_ids * capacity + slot_index
    places = jnp.arange(experts * capacity, dtype=jnp.int32)
    matches = target[None, :, :] == places[:, None, None]
    dispatch = jnp.any(matches, axis=2).astype(jnp.bfloat16)
    outgoing = jnp.dot(dispatch, tokens, preferred_element_type=jnp.float32).astype(jnp.bfloat16)
    outgoing = outgoing.reshape(experts, capacity, tokens.shape[1])
    arrived = lax.all_to_all(outgoing, ("dp", "expert"), split_axis=0, concat_axis=0, tiled=True)
    expert_in = lax.all_gather(arrived, "tensor", axis=2, tiled=True)
    row_count = experts * capacity
    layout_ids = topology[0]
    local_blocks = layout_ids.shape[0]
    blocked = expert_in.reshape(row_count, D // BLK, BLK)
    width_ids = jnp.arange(D // BLK, dtype=jnp.int32)
    partial_value = jnp.zeros((row_count, D // BLK, BLK), jnp.float32)
    for block in range(local_blocks):
        chosen = layout_ids[block]
        picked = jnp.take(blocked, chosen, axis=1)
        gate_proj = jnp.einsum(
            "rkc,kcf->rf", picked, gate_blocks[0, block], preferred_element_type=jnp.float32
        )
        up_proj = jnp.einsum(
            "rkc,kcf->rf", picked, up_blocks[0, block], preferred_element_type=jnp.float32
        )
        hidden = (jax.nn.silu(gate_proj) * up_proj).astype(jnp.bfloat16)
        pieces = jnp.einsum(
            "rf,kfc->rkc", hidden, down_blocks[0, block], preferred_element_type=jnp.float32
        )
        placer = (chosen[:, None] == width_ids[None, :]).astype(jnp.float32)
        partial_value = partial_value + jnp.einsum(
            "rkc,kb->rbc", pieces, placer, precision=lax.Precision.HIGHEST
        )
    partial_low = lax.optimization_barrier(
        partial_value.reshape(experts, capacity, D).astype(jnp.bfloat16)
    )
    shares = lax.all_to_all(
        partial_low.reshape(1, experts, capacity, D),
        "tensor",
        split_axis=3,
        concat_axis=0,
        tiled=True,
    )
    summed = jnp.sum(shares.astype(jnp.float32), axis=0)
    returned_rows = lax.all_to_all(
        summed, ("dp", "expert"), split_axis=0, concat_axis=0, tiled=True
    )
    flat_rows = returned_rows.reshape(row_count, returned_rows.shape[2])
    combined = combine_rows(flat_rows, target, combine_weights)
    return combined.astype(jnp.bfloat16)


def solution(mesh):
    return jax.shard_map(
        per_device,
        mesh=mesh,
        in_specs=(
            P(("dp", "expert"), "tensor"),
            P(("dp", "expert"), None),
            P(("dp", "expert"), None),
            P(("dp", "expert"), "tensor", None),
            P(("dp", "expert"), "tensor", None, None, None),
            P(("dp", "expert"), "tensor", None, None, None),
            P(("dp", "expert"), "tensor", None, None, None),
        ),
        out_specs=P(("dp", "expert"), "tensor"),
        check_vma=False,
    )
```

profile of v0, /device:TPU:1, one launch (start us, length us, event | category | flops | bytes accessed | tf_op | source)
XLA Modules:
  0.0 545.4 jit_solution(15346772995551788982)
XLA Ops:
  9.7 1.8 convolution_convert_fusion
  11.5 2.5 reshape.63
  14.0 73.0 %all_to_all.19 = bf16[128,6,1024]{2,1,0:T(8,128)(2,1)} all-to-all(bf16[128,6,1024]{2,1,0:T(8,128)(2,1)S(1)} %reshape.63), channel_id=1, replica_groups=mesh['dp'=16,'expert'=8,'tensor'=4] {'dp','expert'}, dimensions={0} | all-to-all | bytes 3145728 | tf_op jit(solution)/shard_map/all_to_all | solution.py:37
  87.0 81.0 %all-gather.2.cloned.1.call-done = bf16[128,6,4096]{2,1,0:T(8,128)(2,1)} async-done(((bf16[128,6,1024]{2,1,0:T(8,128)(2,1)}), bf16[128,6,4096]{2,1,0:T(8,128)(2,1)}) %all-gather.2.cloned.1.call-update) | async-done | bytes 6291472 | tf_op jit(solution)/shard_map/all_gather | solution.py:38
  168.1 13.8 %reshape.64 = bf16[768,32,128]{2,1,0:T(8,128)(2,1)} reshape(bf16[128,6,4096]{2,1,0:T(8,128)(2,1)} %all-gather.2.cloned.1.call-done) | data formatting | bytes 12582912 | tf_op jit(solution)/shard_map/reshape | solution.py:42
  181.9 7.9 %copy.83 = bf16[768,32,128]{2,0,1:T(8,128)(2,1)} copy(bf16[768,32,128]{2,1,0:T(8,128)(2,1)} %reshape.64) | data formatting | bytes 12582912 | tf_op jit(solution)/shard_map/reshape | solution.py:42
  189.7 5.2 gather_fusion.1
  194.9 3.8 gather_fusion.2
  198.7 2.5 fusion.28
  201.2 1.8 fusion.34
  203.0 6.5 %fusion.71 = f32[768,12,128]{2,0,1:T(8,128)} fusion(bf16[12,768,128]{2,1,0:T(8,128)(2,1)} %gather_fusion.1, pred[12]{0:T(512)(128)(4,1)S(1)} %get-tuple-element.56, bf16[1,3,12,128,128]{4,3,2,1,0:T(8,128)(2,1)} %param.17, bf16[1,3,12,128,128]{4,3,2,1,0:T(8,128)(2,1)} %param.16, f32[768,128]{1,0:T(8,128)S(1)} %fusion.28), kind=kOutput, calls=%fused_computation.54 | convolution fusion | flops 605749248 | bytes 8257548 | tf_op jit(solution)/shard_map/rf,kfc->rkc/dot_general | solution.py:55
  209.5 5.8 %fusion.74 = f32[768,12,128]{2,0,1:T(8,128)} fusion(bf16[12,768,128]{2,1,0:T(8,128)(2,1)S(1)} %gather_fusion.2, pred[12]{0:T(512)(128)(4,1)S(1)} %get-tuple-element.54, bf16[1,3,12,128,128]{4,3,2,1,0:T(8,128)(2,1)} %param.17, bf16[1,3,12,128,128]{4,3,2,1,0:T(8,128)(2,1)} %param.16, f32[768,128]{1,0:T(8,128)S(1)} %fusion.34), kind=kOutput, calls=%fused_computation.55 | convolution fusion | flops 605749248 | bytes 8257548 | tf_op jit(solution)/shard_map/rf,kfc->rkc/dot_general | solution.py:55
  215.3 3.8 gather_fusion
  219.1 1.4 copy-done.2
  220.5 1.8 fusion.22
  222.3 6.6 %fusion.68 = f32[768,12,128]{2,0,1:T(8,128)} fusion(bf16[12,768,128]{2,1,0:T(8,128)(2,1)} %copy-done.2, pred[12]{0:T(512)(128)(4,1)S(1)} %get-tuple-element.23, bf16[1,3,12,128,128]{4,3,2,1,0:T(8,128)(2,1)} %param.17, bf16[1,3,12,128,128]{4,3,2,1,0:T(8,128)(2,1)} %param.16, f32[768,128]{1,0:T(8,128)S(1)} %fusion.22), kind=kOutput, calls=%fused_computation.53 | convolution fusion | flops 605749248 | bytes 8257548 | tf_op jit(solution)/shard_map/rf,kfc->rkc/dot_general | solution.py:55
  229.0 13.8 %fusion.3 = f32[32,768,128]{2,0,1:T(8,128)} fusion(f32[768,12,128]{2,0,1:T(8,128)} %fusion.71, s32[12]{0:T(128)S(1)} %get-tuple-element.53), kind=kOutput, calls=%fused_computation.16 | convolution fusion | flops 452985216 | bytes 17301552 | tf_op jit(solution)/shard_map/rkc,kb->rbc/dot_general | solution.py:59
  242.7 12.7 %fusion.1 = f32[32,768,128]{2,0,1:T(8,128)} fusion(f32[768,12,128]{2,0,1:T(8,128)S(1)} %bitcast.217, s32[12]{0:T(128)S(1)} %get-tuple-element.52), kind=kOutput, calls=%fused_computation.14 | convolution fusion | flops 452985216 | bytes 17301552 | tf_op jit(solution)/shard_map/rkc,kb->rbc/dot_general | solution.py:59
  255.5 17.1 %fusion = bf16[768,32,128]{2,1,0:T(8,128)(2,1)} fusion(f32[32,768,128]{2,0,1:T(8,128)} %fusion.1, f32[32,768,128]{2,0,1:T(8,128)} %fusion.3, f32[768,12,128]{2,0,1:T(8,128)S(1)} %bitcast.215, s32[12]{0:T(128)S(1)} %get-tuple-element.51), kind=kOutput, calls=%fused_computation.13 | convolution fusion | flops 462422400 | bytes 36175920 | tf_op jit(solution)/shard_map/rkc,kb->rbc/dot_general | solution.py:59
  272.6 13.3 %convert_element_type.51 = bf16[128,6,4096]{2,1,0:T(8,128)(2,1)} reshape(bf16[768,32,128]{2,1,0:T(8,128)(2,1)} %fusion) | data formatting | bytes 12582912 | tf_op jit(solution)/shard_map/convert_element_type | solution.py:63
  285.9 12.8 %copy.89 = bf16[1,128,6,4096]{1,2,0,3:T(8,128)(2,1)} copy(bf16[1,128,6,4096]{3,2,1,0:T(8,128)(2,1)} %bitcast.213) | data formatting | bytes 12582912 | tf_op jit(solution)/shard_map/reshape | solution.py:66
  298.7 96.9 %all_to_all.20 = bf16[1,128,6,4096]{1,2,0,3:T(8,128)(2,1)S(1)} all-to-all(bf16[1,128,6,4096]{1,2,0,3:T(8,128)(2,1)} %copy.89), channel_id=1, replica_groups=mesh['dp'=16,'expert'=8,'tensor'=4] {'tensor'}, dimensions={3} | all-to-all | bytes 12582912 | tf_op jit(solution)/shard_map/all_to_all | solution.py:65
  395.6 3.5 copy.90
  399.1 4.1 convert_reduce_fusion
  403.1 3.5 copy.91
  406.6 16.1 %all-to-all-start.2 = ((f32[128,6,1024]{2,1,0:T(8,128)}), f32[128,6,1024]{2,1,0:T(8,128)}, u32[]{:S(2)}, u32[]{:S(2)}) async-start(f32[128,6,1024]{2,1,0:T(8,128)} %copy.91), calls=%async_computation.2 | async-start | bytes 8388608 | tf_op jit(solution)/shard_map/all_to_all | solution.py:73
  424.0 98.6 %all-to-all-done.2 = f32[128,6,1024]{2,1,0:T(8,128)} async-done(((f32[128,6,1024]{2,1,0:T(8,128)}), f32[128,6,1024]{2,1,0:T(8,128)}, u32[]{:S(2)}, u32[]{:S(2)}) %all-to-all-start.2) | async-done | bytes 3145760 | tf_op jit(solution)/shard_map/all_to_all | solution.py:73
  522.6 3.1 reshape.66
  526.3 1.4 gather_fusion.4
  529.1 1.4 gather_fusion.6
  530.4 1.4 gather_fusion.7
  535.9 2.4 fusion.118
  (55 shorter events, 10.5 us)
Async XLA Ops:
  6.5 3.2 copy-start
  6.5 161.6 %all-gather.2.cloned.1.call-start = ((), (), s32[]{:S(2)}) async-start(), calls=%async_computation.3 | async-start | bytes 10485760 | tf_op jit(solution)/shard_map/all_gather | solution.py:38
  14.0 73.0 %copy-start.3 = (s32[1,3,12]{2,0,1:T(1,128)S(1)}, s32[1,3,12]{2,0,1:T(1,128)}, u32[]{:S(2)}) copy-start(s32[1,3,12]{2,0,1:T(1,128)} %param.14) | copy-start | bytes 436
  219.1 1.4 copy-start.2
  222.3 20.4 %slice-start.2 = ((s8[4718592]{0:T(1024)(128)(4,1)}), s8[524288]{0:T(1024)(128)(4,1)S(1)}, s32[]{:S(2)}) async-start(s8[4718592]{0:T(1024)(128)(4,1)} %bitcast.216), calls=%async_computation.6 | async-start | bytes 1048576
  228.9 13.8 %slice-start.3 = ((s8[4718592]{0:T(1024)(128)(4,1)}), s8[4194304]{0:T(1024)(128)(4,1)S(1)}, s32[]{:S(2)}) async-start(s8[4718592]{0:T(1024)(128)(4,1)} %bitcast.216), calls=%async_computation.7 | async-start | bytes 8388608
  229.0 26.5 %slice-start = ((s8[4718592]{0:T(1024)(128)(4,1)}), s8[4194304]{0:T(1024)(128)(4,1)S(1)}, s32[]{:S(2)}) async-start(s8[4718592]{0:T(1024)(128)(4,1)} %bitcast.214), calls=%async_computation.4 | async-start | bytes 8388608
  242.7 12.8 %slice-start.1 = ((s8[4718592]{0:T(1024)(128)(4,1)}), s8[524288]{0:T(1024)(128)(4,1)S(1)}, s32[]{:S(2)}) async-start(s8[4718592]{0:T(1024)(128)(4,1)} %bitcast.214), calls=%async_computation.5 | async-start | bytes 1048576
  406.6 16.8 %copy-start.4 = (f32[64,8]{0,1:T(8,128)S(1)}, f32[64,8]{0,1:T(8,128)}, u32[]{:S(2)}) copy-start(f32[64,8]{0,1:T(8,128)} %param.13) | copy-start | bytes 6148
  406.6 116.0 %all-to-all-start.2 = ((f32[128,6,1024]{2,1,0:T(8,128)}), f32[128,6,1024]{2,1,0:T(8,128)}, u32[]{:S(2)}, u32[]{:S(2)}) async-start(f32[128,6,1024]{2,1,0:T(8,128)} %copy.91), calls=%async_computation.2 | async-start | bytes 8388608 | tf_op jit(solution)/shard_map/all_to_all | solution.py:73
  533.2 5.1 copy-start.1
  534.6 1.4 copy-start.5
Sparse Core Ops, SparseCore 0:
  87.1 80.9 all-gather.1
where the time goes:
time: 550 us; the launch traced here: 545 us
  waiting for transfers between devices  180 us (33%)
  blocking collectives  170 us (31%)
  local copies, waits for them, and re-layouts  86.6 us (16%)
  matrix products  70.4 us (13%)
  starting transfers between devices  16.1 us (3%)
  between operations  13.9 us (3%)
  other arithmetic  8.84 us (2%)
    all_to_all x1, waiting for transfers between devices, per_device(): lax.all_to_all(summed, ('dp', 'expert'), split_axis=0, concat_axis=0, til...  98.6 us
    all_to_all x1, blocking collectives, per_device(): lax.all_to_all(partial_low.reshape(1, experts, capacity, D), 'tensor', sp...  96.9 us
    all_gather x1, waiting for transfers between devices, per_device(): expert_in = lax.all_gather(arrived, 'tensor', axis=2, tiled=True)  81 us
    all_to_all x1, blocking collectives, per_device(): lax.all_to_all(outgoing, ('dp', 'expert'), split_axis=0, concat_axis=0, t...  73 us
    dot_general x3, matrix products, per_device(): jnp.einsum('rkc,kb->rbc', pieces, placer, precision=lax.Precision.HIGHEST)  43.6 us
    reshape x2, local copies, waits for them, and re-layouts, per_device(): blocked = expert_in.reshape(row_count, D // BLK, BLK)  21.6 us
    dot_general x3, matrix products, per_device(): jnp.einsum('rf,kfc->rkc', hidden, down_blocks[0, block], preferred_elemen...  18.9 us
    all_to_all x1, starting transfers between devices, per_device(): lax.all_to_all(summed, ('dp', 'expert'), split_axis=0, concat_axis=0, til...  16.1 us
  transfers between devices with their start and end apart: 2, of which 2 were waited for; matrix products, arithmetic and copies ran while one was open for 0% of the time, Pallas kernels for 0%

commit v1 on v0

--- a/solution.py
+++ b/solution.py
@@ -62,12 +62,18 @@
     partial_low = lax.optimization_barrier(
         partial_value.reshape(experts, capacity, D).astype(jnp.bfloat16)
     )
-    shares = lax.all_to_all(
-        partial_low.reshape(1, experts, capacity, D),
-        "tensor",
-        split_axis=3,
-        concat_axis=0,
-        tiled=True,
+    shares = jnp.concatenate(
+        lax.all_to_all(
+            jnp.stack(
+                jnp.split(
+                    partial_low.reshape(1, experts, capacity, D), lax.axis_size("tensor"), axis=3
+                )
+            ),
+            "tensor",
+            0,
+            0,
+        ),
+        axis=0,
     )
     summed = jnp.sum(shares.astype(jnp.float32), axis=0)
     returned_rows = lax.all_to_all(

time: 550 us -> 522 us (0.949)
  blocking collectives: 170 us -> 147 us
  local copies, waits for them, and re-layouts: 86.6 us -> 80.9 us
    all_to_all x1, blocking collectives: 96.9 us -> 74.5 us  [per_device(): lax.all_to_all(jnp.stack(jnp.split(partial_low.reshape(1, experts, capaci...]
    reshape x1 -> x0, local copies, waits for them, and re-layouts: 12.8 us -> none  [per_device(): partial_low.reshape(1, experts, capacity, D)]
    another operation x3 -> x5, local copies, waits for them, and re-layouts: 0.03 us -> 10.1 us  [the longest x2 10.1 us: per_device(): jnp.stack(jnp.split(partial_low.reshape(1, experts, capacity, D), lax.axi...]
where the time goes in v1:
time: 522 us; the launch traced here: 517 us
  waiting for transfers between devices  180 us (34%)
  blocking collectives  147 us (28%)
  local copies, waits for them, and re-layouts  80.9 us (15%)
  matrix products  70.9 us (14%)
  starting transfers between devices  16.1 us (3%)
  between operations  13.9 us (3%)
  other arithmetic  8.53 us (2%)
    all_to_all x1, waiting for transfers between devices, per_device(): lax.all_to_all(summed, ('dp', 'expert'), split_axis=0, concat_axis=0, til...  98.6 us
    all_gather x1, waiting for transfers between devices, per_device(): expert_in = lax.all_gather(arrived, 'tensor', axis=2, tiled=True)  81 us
    all_to_all x1, blocking collectives, per_device(): lax.all_to_all(jnp.stack(jnp.split(partial_low.reshape(1, experts, capaci...  74.5 us
    all_to_all x1, blocking collectives, per_device(): lax.all_to_all(outgoing, ('dp', 'expert'), split_axis=0, concat_axis=0, t...  72.8 us
    dot_general x3, matrix products, per_device(): jnp.einsum('rkc,kb->rbc', pieces, placer, precision=lax.Precision.HIGHEST)  44.1 us
    reshape x2, local copies, waits for them, and re-layouts, per_device(): blocked = expert_in.reshape(row_count, D // BLK, BLK)  21.6 us
    dot_general x3, matrix products, per_device(): jnp.einsum('rf,kfc->rkc', hidden, down_blocks[0, block], preferred_elemen...  18.9 us
    all_to_all x1, starting transfers between devices, per_device(): lax.all_to_all(summed, ('dp', 'expert'), split_axis=0, concat_axis=0, til...  16.1 us
  transfers between devices with their start and end apart: 2, of which 2 were waited for; matrix products, arithmetic and copies ran while one was open for 0% of the time, Pallas kernels for 0%

profile of v1, /device:TPU:1, one launch (start us, length us, event | category | flops | bytes accessed | tf_op | source)
XLA Modules:
  0.0 517.3 jit_solution(11604110290503287347)
XLA Ops:
  9.7 1.8 convolution_convert_fusion
  11.5 2.5 reshape.61
  14.0 72.8 %all_to_all.15 = bf16[128,6,1024]{2,1,0:T(8,128)(2,1)} all-to-all(bf16[128,6,1024]{2,1,0:T(8,128)(2,1)S(1)} %reshape.61), channel_id=1, replica_groups=mesh['dp'=16,'expert'=8,'tensor'=4] {'dp','expert'}, dimensions={0} | all-to-all | bytes 3145728 | tf_op jit(solution)/shard_map/all_to_all | solution.py:37
  86.9 81.0 %all-gather.2.cloned.1.call-done = bf16[128,6,4096]{2,1,0:T(8,128)(2,1)} async-done(((bf16[128,6,1024]{2,1,0:T(8,128)(2,1)}), bf16[128,6,4096]{2,1,0:T(8,128)(2,1)}) %all-gather.2.cloned.1.call-update) | async-done | bytes 6291472 | tf_op jit(solution)/shard_map/all_gather | solution.py:38
  167.9 13.8 %reshape.62 = bf16[768,32,128]{2,1,0:T(8,128)(2,1)} reshape(bf16[128,6,4096]{2,1,0:T(8,128)(2,1)} %all-gather.2.cloned.1.call-done) | data formatting | bytes 12582912 | tf_op jit(solution)/shard_map/reshape | solution.py:42
  181.7 7.9 %copy.91 = bf16[768,32,128]{2,0,1:T(8,128)(2,1)} copy(bf16[768,32,128]{2,1,0:T(8,128)(2,1)} %reshape.62) | data formatting | bytes 12582912 | tf_op jit(solution)/shard_map/reshape | solution.py:42
  189.6 5.2 %gather_fusion.1 = bf16[12,768,128]{2,1,0:T(8,128)(2,1)} fusion(bf16[768,32,128]{2,0,1:T(8,128)(2,1)} %copy.91, s32[1024]{0:T(1024)S(1)} %get-tuple-element.63), kind=kCustom, calls=%fused_computation.2.clone | custom fusion | bytes 4718640 | tf_op jit(solution)/shard_map/jit(_take)/gather | solution.py:47
  194.7 3.8 gather_fusion.2
  198.5 2.5 fusion.28
  201.1 1.8 fusion.34
  202.9 6.5 %fusion.71 = f32[768,12,128]{2,0,1:T(8,128)} fusion(bf16[12,768,128]{2,1,0:T(8,128)(2,1)} %gather_fusion.1, pred[12]{0:T(512)(128)(4,1)S(1)} %get-tuple-element.60, bf16[1,3,12,128,128]{4,3,2,1,0:T(8,128)(2,1)} %param.17, bf16[1,3,12,128,128]{4,3,2,1,0:T(8,128)(2,1)} %param.16, f32[768,128]{1,0:T(8,128)S(1)} %fusion.28), kind=kOutput, calls=%fused_computation.59 | convolution fusion | flops 605749248 | bytes 8257548 | tf_op jit(solution)/shard_map/rf,kfc->rkc/dot_general | solution.py:55
  209.3 5.8 %fusion.74 = f32[768,12,128]{2,0,1:T(8,128)} fusion(bf16[12,768,128]{2,1,0:T(8,128)(2,1)S(1)} %gather_fusion.2, pred[12]{0:T(512)(128)(4,1)S(1)} %get-tuple-element.58, bf16[1,3,12,128,128]{4,3,2,1,0:T(8,128)(2,1)} %param.17, bf16[1,3,12,128,128]{4,3,2,1,0:T(8,128)(2,1)} %param.16, f32[768,128]{1,0:T(8,128)S(1)} %fusion.34), kind=kOutput, calls=%fused_computation.60 | convolution fusion | flops 605749248 | bytes 8257548 | tf_op jit(solution)/shard_map/rf,kfc->rkc/dot_general | solution.py:55
  215.1 3.8 gather_fusion
  218.9 1.4 copy-done.2
  220.4 1.8 fusion.22
  222.2 6.6 %fusion.68 = f32[768,12,128]{2,0,1:T(8,128)} fusion(bf16[12,768,128]{2,1,0:T(8,128)(2,1)} %copy-done.2, pred[12]{0:T(512)(128)(4,1)S(1)} %get-tuple-element.23, bf16[1,3,12,128,128]{4,3,2,1,0:T(8,128)(2,1)} %param.17, bf16[1,3,12,128,128]{4,3,2,1,0:T(8,128)(2,1)} %param.16, f32[768,128]{1,0:T(8,128)S(1)} %fusion.22), kind=kOutput, calls=%fused_computation.58 | convolution fusion | flops 605749248 | bytes 8257548 | tf_op jit(solution)/shard_map/rf,kfc->rkc/dot_general | solution.py:55
  228.8 14.2 %fusion.3 = f32[32,768,128]{2,0,1:T(8,128)} fusion(f32[768,12,128]{2,0,1:T(8,128)} %fusion.71, s32[12]{0:T(128)S(1)} %get-tuple-element.57), kind=kOutput, calls=%fused_computation.17 | convolution fusion | flops 452985216 | bytes 17301552 | tf_op jit(solution)/shard_map/rkc,kb->rbc/dot_general | solution.py:59
  243.1 12.7 %fusion.1 = f32[32,768,128]{2,0,1:T(8,128)} fusion(f32[768,12,128]{2,0,1:T(8,128)S(1)} %bitcast.223, s32[12]{0:T(128)S(1)} %get-tuple-element.56), kind=kOutput, calls=%fused_computation.15 | convolution fusion | flops 452985216 | bytes 17301552 | tf_op jit(solution)/shard_map/rkc,kb->rbc/dot_general | solution.py:59
  255.8 17.1 %fusion = bf16[768,32,128]{2,1,0:T(8,128)(2,1)} fusion(f32[32,768,128]{2,0,1:T(8,128)} %fusion.1, f32[32,768,128]{2,0,1:T(8,128)} %fusion.3, f32[768,12,128]{2,0,1:T(8,128)S(1)} %bitcast.221, s32[12]{0:T(128)S(1)} %get-tuple-element.55), kind=kOutput, calls=%fused_computation.14 | convolution fusion | flops 462422400 | bytes 36175920 | tf_op jit(solution)/shard_map/rkc,kb->rbc/dot_general | solution.py:59
  272.9 13.3 %convert_element_type.47 = bf16[128,6,4096]{2,1,0:T(8,128)(2,1)} reshape(bf16[768,32,128]{2,1,0:T(8,128)(2,1)} %fusion) | data formatting | bytes 12582912 | tf_op jit(solution)/shard_map/convert_element_type | solution.py:63
  286.2 3.9 slice_bitcast_fusion.3
  290.1 2.3 pad_maximum_fusion
  292.3 6.2 %copy.97 = bf16[4,1,128,6,1024]{4,2,3,1,0:T(8,128)(2,1)} copy(bf16[4,1,128,6,1024]{4,3,2,1,0:T(8,128)(2,1)S(1)} %pad_maximum_fusion) | data formatting | bytes 12582912 | tf_op jit(solution)/shard_map/stack | solution.py:67
  298.5 74.5 %all_to_all.16 = bf16[4,1,128,6,1024]{4,2,3,1,0:T(8,128)(2,1)S(1)} all-to-all(bf16[4,1,128,6,1024]{4,2,3,1,0:T(8,128)(2,1)} %copy.97), channel_id=1, replica_groups=mesh['dp'=16,'expert'=8,'tensor'=4] {'tensor'}, dimensions={0} | all-to-all | bytes 12582912 | tf_op jit(solution)/shard_map/all_to_all | solution.py:66
  373.0 1.5 convert_reduce_fusion
  374.5 3.9 copy.98
  378.4 16.1 %all-to-all-start.2 = ((f32[128,6,1024]{2,1,0:T(8,128)}), f32[128,6,1024]{2,1,0:T(8,128)}, u32[]{:S(2)}, u32[]{:S(2)}) async-start(f32[128,6,1024]{2,1,0:T(8,128)} %copy.98), calls=%async_computation.2 | async-start | bytes 8388608 | tf_op jit(solution)/shard_map/all_to_all | solution.py:79
  395.7 98.6 %all-to-all-done.2 = f32[128,6,1024]{2,1,0:T(8,128)} async-done(((f32[128,6,1024]{2,1,0:T(8,128)}), f32[128,6,1024]{2,1,0:T(8,128)}, u32[]{:S(2)}, u32[]{:S(2)}) %all-to-all-start.2) | async-done | bytes 3145760 | tf_op jit(solution)/shard_map/all_to_all | solution.py:79
  494.4 3.1 reshape.64
  500.9 1.4 gather_fusion.6
  502.2 1.4 gather_fusion.7
  507.8 2.4 fusion.118
  (56 shorter events, 12.0 us)
Async XLA Ops:
  6.5 3.2 copy-start
  6.5 161.4 %all-gather.2.cloned.1.call-start = ((), (), s32[]{:S(2)}) async-start(), calls=%async_computation.3 | async-start | bytes 10485760 | tf_op jit(solution)/shard_map/all_gather | solution.py:38
  14.0 72.8 %copy-start.3 = (s32[1,3,12]{2,0,1:T(1,128)S(1)}, s32[1,3,12]{2,0,1:T(1,128)}, u32[]{:S(2)}) copy-start(s32[1,3,12]{2,0,1:T(1,128)} %param.14) | copy-start | bytes 436
  218.9 1.4 copy-start.2
  222.2 20.9 %slice-start.2 = ((s8[4718592]{0:T(1024)(128)(4,1)}), s8[524288]{0:T(1024)(128)(4,1)S(1)}, s32[]{:S(2)}) async-start(s8[4718592]{0:T(1024)(128)(4,1)} %bitcast.222), calls=%async_computation.6 | async-start | bytes 1048576
  228.8 14.3 %slice-start.3 = ((s8[4718592]{0:T(1024)(128)(4,1)}), s8[4194304]{0:T(1024)(128)(4,1)S(1)}, s32[]{:S(2)}) async-start(s8[4718592]{0:T(1024)(128)(4,1)} %bitcast.222), calls=%async_computation.7 | async-start | bytes 8388608
  228.8 27.0 %slice-start = ((s8[4718592]{0:T(1024)(128)(4,1)}), s8[4194304]{0:T(1024)(128)(4,1)S(1)}, s32[]{:S(2)}) async-start(s8[4718592]{0:T(1024)(128)(4,1)} %bitcast.220), calls=%async_computation.4 | async-start | bytes 8388608
  243.1 12.8 %slice-start.1 = ((s8[4718592]{0:T(1024)(128)(4,1)}), s8[524288]{0:T(1024)(128)(4,1)S(1)}, s32[]{:S(2)}) async-start(s8[4718592]{0:T(1024)(128)(4,1)} %bitcast.220), calls=%async_computation.5 | async-start | bytes 1048576
  378.4 16.7 %copy-start.4 = (f32[64,8]{0,1:T(8,128)S(1)}, f32[64,8]{0,1:T(8,128)}, u32[]{:S(2)}) copy-start(f32[64,8]{0,1:T(8,128)} %param.13) | copy-start | bytes 6148
  378.4 116.0 %all-to-all-start.2 = ((f32[128,6,1024]{2,1,0:T(8,128)}), f32[128,6,1024]{2,1,0:T(8,128)}, u32[]{:S(2)}, u32[]{:S(2)}) async-start(f32[128,6,1024]{2,1,0:T(8,128)} %copy.98), calls=%async_computation.2 | async-start | bytes 8388608 | tf_op jit(solution)/shard_map/all_to_all | solution.py:79
  505.0 5.2 copy-start.1
  506.4 1.4 copy-start.5
Sparse Core Ops, SparseCore 0:
  86.9 80.9 all-gather.1
